TPU v7x, 32 devices: a whole 2x2x4 slice. The times are simulated.
32 devices in a mesh: ia: 4 (over z), ja: 4 (over y, x), ka: 2 (over core).
Axes of the slice: x: 2, y: 2, z: 4, core: 2. Of those that a mesh axis runs over, the one named last changes fastest.
Arguments:
- blocks: bfloat16 [4, 4, 4, 128, 128, 128], P('ia', 'ja', 'ka'), may hold values from -6 to 6
- coordinates: int32 [3, 4, 4, 4], P(None, 'ia', 'ja', 'ka'), may hold values from 0 to 3, as said below
- occupancy: int32 [4, 4, 4], P('ia', 'ja', 'ka'), may hold values from 0 to 1, as said below
- second_factor: bfloat16 [4, 512, 1024], P('ja', ('ia', 'ka')), may hold values from -12 to 12
- third_factor: bfloat16 [2, 512, 1024], P('ka', ('ia', 'ja')), may hold values from -0.0234375 to 0.0234375
- inverse_first: bfloat16 [1024, 1024], replicated
- inverse_second: bfloat16 [1024, 1024], replicated
Outputs:
- first_new: bfloat16 [4, 512, 1024], P('ia', ('ja', 'ka'))
- second_new: bfloat16 [4, 512, 1024], P('ja', ('ia', 'ka'))
Inputs may be any that keep to these rules, and one draw needn't show every extreme that they name: `occupancy`: each device has two slots; its second slot is occupied only where its first is. A device with two blocks is followed along ka, cyclically, by a device with none. Some device holds two blocks. coordinates[0], [1], [2] of a slot are a block row among 4, a block row among 4 and a block layer among 4 of its device's ranges; the two slots of a device name different layers.
All inputs are finite; a program needn't handle non-finite values.
Results may differ from a plain program's by a relative error of at most 0.006.
Values may be sent and summed in bfloat16 or wider, within the bound.
A program may use at most 128 MiB of HBM per device.

v0:
```python
import functools

import jax
import jax.numpy as jnp
from jax import lax
from jax.experimental import pallas as pl
from jax.experimental.pallas import tpu as pltpu
from jax.sharding import PartitionSpec as P

IB = 4
JB = 4
TILES = 4
MESH = pl.DeviceIdType.MESH
AXES = ("ia", "ja", "ka")


def kernel(
    sizes,
    blocks,
    places_in,
    occupied_in,
    second_in,
    third_in,
    inverse_first,
    inverse_second,
    first_out,
    second_out,
    xbuf,
    inv1,
    inv2,
    meta_s,
    meta_r,
    cbuf,
    bbuf,
    slab_s,
    slab_r,
    cuse,
    buse,
    tbuf,
    oacc,
    d1s,
    d1r,
    keep1,
    p1s,
    p1r,
    own1,
    fr1,
    abuf,
    d2s,
    d2r,
    keep2,
    p2s,
    p2r,
    own2,
    fr2,
    places,
    occupied,
    local_sem,
    once_send,
    once_recv,
    z_send,
    z_recv,
    y_send,
    y_recv,
    k_send,
    k_recv,
):
    na, nb, nc = sizes
    tiles, edge, width = slab_s.shape
    rs, rt = bbuf.shape[3], cbuf.shape[3]
    sh1, sh2 = abuf.shape[3], own2.shape[1]
    a, b, c = (lax.axis_index(name) for name in AXES)
    sent = []

    def away(axis, d):
        n = sizes[AXES.index(axis)]
        me = (a, b, c)[AXES.index(axis)]
        return lax.rem(me + d, n)

    def send(src, dst, send_sem, recv_sem, axis, d):
        copy = pltpu.make_async_remote_copy(
            src_ref=src,
            dst_ref=dst,
            send_sem=send_sem,
            recv_sem=recv_sem,
            device_id={axis: away(axis, d)},
            device_id_type=MESH,
        )
        copy.start()
        sent.append(copy)
        return copy

    def cols(t):
        return pl.ds(t * width, width)

    local = []

    def local_copy(src, dst):
        copy = pltpu.make_async_copy(src, dst, local_sem.at[len(local)])
        copy.start()
        local.append(copy)
        return copy

    got_places = local_copy(places_in, places)
    got_occupied = local_copy(occupied_in, occupied)
    own_third = [
        local_copy(third_in.at[0, :, cols(t)], cbuf.at[t, a, b]) for t in range(tiles)
    ]
    own_second = [
        local_copy(second_in.at[0, :, cols(t)], bbuf.at[t, a, c]) for t in range(tiles)
    ]
    own_block = local_copy(blocks.at[0, 0, 0], xbuf.at[0])
    got_inv1 = local_copy(inverse_first, inv1)
    got_inv2 = local_copy(inverse_second, inv2)

    barrier = pltpu.get_barrier_semaphore()
    for axis, n in zip(AXES, sizes):
        for d in range(1, n):
            pl.semaphore_signal(
                barrier, inc=1, device_id={axis: away(axis, d)}, device_id_type=MESH
            )
    got_places.wait()
    got_occupied.wait()
    keep = occupied[0, 0, 0] > 0
    row0, col0, layer0 = (places[m, 0, 0, 0] for m in range(3))
    row1, col1, layer1 = (places[m, 0, 0, 1] for m in range(3))
    weight1 = jnp.where(occupied[0, 0, 1] > 0, 1.0, 0.0).astype(jnp.float32)
    for q in range(IB):
        value = jnp.where(row1 == q, weight1, 0.0)
        meta_s[pl.ds(q, 1), :] = jnp.full((1, width), value, jnp.float32)
    for q in range(JB):
        value = jnp.where(col1 == q, weight1, 0.0)
        meta_s[pl.ds(IB + q, 1), :] = jnp.full((1, width), value, jnp.float32)
    pl.semaphore_wait(barrier, (na - 1) + (nb - 1) + (nc - 1))

    def chosen(own_value, row):
        own = jnp.where(own_value, 1.0, 0.0).astype(jnp.float32)
        return jnp.where(keep, jnp.full((1, width), own, jnp.float32), meta_r[pl.ds(row, 1), :]) > 0.5

    def third_column(t):
        return [
            send(
                third_in.at[0, :, cols(t)],
                cbuf.at[t, a, b],
                z_send.at[0, t, d - 1],
                z_recv.at[0, t, d - 1],
                "ia",
                d,
            )
            for d in range(1, na)
        ]

    def second_column(t):
        return [
            send(
                second_in.at[0, :, cols(t)],
                bbuf.at[t, a, c],
                z_send.at[1, t, d - 1],
                z_recv.at[1, t, d - 1],
                "ia",
                d,
            )
            for d in range(1, na)
        ]

    third_z, second_z = {}, {}
    third_z[0] = third_column(0)
    block_copy = send(blocks.at[0, 0, 1], xbuf.at[1], once_send.at[0], once_recv.at[0], "ka", 1)
    meta_copy = send(meta_s, meta_r, once_send.at[1], once_recv.at[1], "ka", 1)
    for t in range(1, tiles):
        third_z[t] = third_column(t)
        second_z[t - 1] = second_column(t - 1)
    second_z[tiles - 1] = second_column(tiles - 1)

    third_y, second_k, slab_copy = {}, {}, {}

    def spread_third(t):
        own_third[t].wait()
        for copy in third_z[t]:
            copy.wait_recv()
        third_y[t] = [
            send(
                cbuf.at[t, :, b],
                cbuf.at[t, :, b],
                y_send.at[0, t, d - 1],
                y_recv.at[0, t, d - 1],
                "ja",
                d,
            )
            for d in range(1, nb)
        ]

    def spread_second(t):
        own_second[t].wait()
        for copy in second_z[t]:
            copy.wait_recv()
        second_k[t] = [
            send(
                bbuf.at[t, :, c],
                bbuf.at[t, :, c],
                k_send.at[0, t, d - 1],
                k_recv.at[0, t, d - 1],
                "ka",
                d,
            )
            for d in range(1, nc)
        ]

    def layer_piece(t, layer, piece):
        per = edge // rt
        total = na * nb * rt // edge
        value = None
        for q in range(total):
            s = q * per + piece
            rows = cbuf[t, s // nb, s % nb]
            value = rows if value is None else jnp.where(layer == q, rows, value)
        return value

    def pass_slab(t):
        for copy in third_y[t]:
            copy.wait_recv()
        for piece in range(edge // rt):
            slab_s[t, pl.ds(piece * rt, rt), :] = layer_piece(t, layer1, piece)
        slab_copy[t] = send(
            slab_s.at[t], slab_r.at[t], k_send.at[1, t, 0], k_recv.at[1, t, 0], "ka", 1
        )
        for piece in range(edge // rt):
            cuse[pl.ds(piece * rt, rt), :] = layer_piece(t, layer0, piece)

    def first_products(t):
        for copy in second_k[t]:
            copy.wait_recv()
        if t == 0:
            own_block.wait()
            block_copy.wait_recv()
            meta_copy.wait_recv()
        masks = [chosen(col0 == q, IB + q) for q in range(JB)]
        per = edge // rs
        for piece in range(per):
            value = jnp.zeros((rs, width), jnp.float32)
            for q in range(JB):
                s = q * per + piece
                rows = bbuf[t, s // nc, s % nc].astype(jnp.float32)
                value = jnp.where(masks[q], rows, value)
            buse[pl.ds(piece * rs, rs), :] = value
        slab_copy[t].wait_recv()
        cuse[...] = jnp.where(keep, cuse[...], slab_r[t])
        slot = jnp.where(keep, 0, 1)

        def eight(step, carry):
            base = pl.multiple_of(step * 8, 8)
            sums = []
            for u in range(8):
                product = jnp.dot(
                    xbuf[slot, base + u], cuse[...], preferred_element_type=jnp.float32
                )
                tbuf[t, base + u] = product.astype(jnp.bfloat16)
                sums.append(jnp.sum(product * buse[...], axis=0, keepdims=True))
            oacc[pl.ds(base, 8), :] = jnp.concatenate(sums, axis=0)
            return carry

        lax.fori_loop(0, edge // 8, eight, 0)

    def owned_piece(owner, rows, own_place, meta_row):
        start = owner * rows
        block = start // edge
        off = pl.multiple_of(start % edge, rows)
        mask = chosen(own_place == block, meta_row + block)
        return jnp.where(mask, oacc[pl.ds(off, rows), :], 0.0)

    def pair_sums(t, n, rows, own_place, meta_row, outgoing, arriving, kept, kind):
        copies = []
        for d in range(1, nc):
            for m in range(n):
                owner = m * nc + away("ka", d)
                outgoing[t, d - 1, m] = owned_piece(owner, rows, own_place, meta_row).astype(
                    jnp.bfloat16
                )
            copies.append(
                send(
                    outgoing.at[t, d - 1],
                    arriving.at[t, d - 1],
                    k_send.at[kind, t, d - 1],
                    k_recv.at[kind, t, d - 1],
                    "ka",
                    d,
                )
            )
        for m in range(n):
            kept[t, m] = owned_piece(m * nc + c, rows, own_place, meta_row)
        return copies

    def chip_sums(t, axis, n, copies, arriving, kept, outgoing, landing, own, sends, recvs, kind):
        for copy in copies:
            copy.wait_recv()
        started = []
        for d in range(n):
            m = away(axis, d)
            value = kept[t, m]
            for e in range(1, nc):
                value = value + arriving[t, e - 1, m].astype(jnp.float32)
            if d == 0:
                own[t] = value
            else:
                outgoing[t, d - 1] = value.astype(jnp.bfloat16)
                started.append(
                    send(
                        outgoing.at[t, d - 1],
                        landing.at[t, d - 1],
                        sends.at[kind, t, d - 1],
                        recvs.at[kind, t, d - 1],
                        axis,
                        d,
                    )
                )
        return started

    first_k, first_y = {}, {}

    def first_chip_sums(t):
        first_y[t] = chip_sums(
            t, "ja", nb, first_k[t], d1r, keep1, p1s, p1r, own1, y_send, y_recv, 1
        )

    spread_third(0)
    spread_second(0)
    for t in range(tiles):
        if t + 1 < tiles:
            spread_third(t + 1)
        pass_slab(t)
        if t:
            first_chip_sums(t - 1)
        first_products(t)
        first_k[t] = pair_sums(t, nb, sh1, row0, 0, d1s, d1r, keep1, 2)
        if t + 1 < tiles:
            spread_second(t + 1)
    first_chip_sums(tiles - 1)

    def gathered(t, copies, own, landing, n):
        for copy in copies:
            copy.wait_recv()
        value = own[t]
        for d in range(1, n):
            value = value + landing[t, d - 1].astype(jnp.float32)
        return value.astype(jnp.bfloat16)

    for t in range(tiles):
        fr1[:, cols(t)] = gathered(t, first_y[t], own1, p1r, nb)
    got_inv1.wait()
    new_y, new_k = {}, {}
    for t in range(tiles):
        value = jnp.dot(fr1[...], inv1[:, cols(t)], preferred_element_type=jnp.float32)
        value = value.astype(jnp.bfloat16)
        abuf[t, b, c] = value
        first_out[0, :, cols(t)] = value
        new_y[t] = [
            send(
                abuf.at[t, b, c],
                abuf.at[t, b, c],
                y_send.at[2, t, d - 1],
                y_recv.at[2, t, d - 1],
                "ja",
                d,
            )
            for d in range(1, nb)
        ]

    def spread_new(t):
        for copy in new_y[t]:
            copy.wait_recv()
        new_k[t] = [
            send(
                abuf.at[t, :, c],
                abuf.at[t, :, c],
                k_send.at[3, t, d - 1],
                k_recv.at[3, t, d - 1],
                "ka",
                d,
            )
            for d in range(1, nc)
        ]

    def second_products(t):
        for copy in new_k[t]:
            copy.wait_recv()
        masks = [chosen(row0 == q, q) for q in range(IB)]
        per = edge // sh1
        for piece in range(per):
            value = jnp.zeros((sh1, width), jnp.float32)
            for q in range(IB):
                s = q * per + piece
                rows = abuf[t, s // nc, s % nc].astype(jnp.float32)
                value = jnp.where(masks[q], rows, value)
            buse[pl.ds(piece * sh1, sh1), :] = value
        lanes = 128
        for lane in range(0, width, lanes):

            def eight(step, total):
                base = pl.multiple_of(step * 8, 8)
                rows = buse[pl.ds(base, 8), pl.ds(lane, lanes)]
                for u in range(8):
                    total = total + rows[u : u + 1] * tbuf[t, base + u, :, pl.ds(lane, lanes)].astype(
                        jnp.float32
                    )
                return total

            oacc[:, pl.ds(lane, lanes)] = lax.fori_loop(
                0, edge // 8, eight, jnp.zeros((edge, lanes), jnp.float32)
            )

    second_s, second_y = {}, {}

    def second_chip_sums(t):
        second_y[t] = chip_sums(
            t, "ia", na, second_s[t], d2r, keep2, p2s, p2r, own2, z_send, z_recv, 2
        )

    spread_new(0)
    for t in range(tiles):
        if t + 1 < tiles:
            spread_new(t + 1)
        second_products(t)
        second_s[t] = pair_sums(t, na, sh2, col0, IB, d2s, d2r, keep2, 4)
        if t:
            second_chip_sums(t - 1)
    second_chip_sums(tiles - 1)
    for t in range(tiles):
        fr2[:, cols(t)] = gathered(t, second_y[t], own2, p2r, na)
    got_inv2.wait()
    for t in range(tiles):
        value = jnp.dot(fr2[...], inv2[:, cols(t)], preferred_element_type=jnp.float32)
        second_out[0, :, cols(t)] = value.astype(jnp.bfloat16)
    for copy in sent:
        copy.wait_send()


def body(
    sizes,
    blocks,
    coordinates,
    occupancy,
    second_factor,
    third_factor,
    inverse_first,
    inverse_second,
):
    na, nb, nc = sizes
    edge, rank = blocks.shape[-1], inverse_first.shape[0]
    tiles = TILES
    width = rank // tiles
    rs, rt = second_factor.shape[1], third_factor.shape[1]
    sh1, sh2 = IB * edge // (nb * nc), JB * edge // (na * nc)
    bf16, f32 = jnp.bfloat16, jnp.float32
    dma = pltpu.SemaphoreType.DMA
    widest_k = max(nc - 1, 1)
    vmem = pl.BlockSpec(memory_space=pltpu.VMEM)
    anywhere = pl.BlockSpec(memory_space=pl.ANY)
    scratch = [
        pltpu.VMEM((2, edge, edge, edge), bf16),
        pltpu.VMEM((rank, rank), bf16),
        pltpu.VMEM((rank, rank), bf16),
        pltpu.VMEM((IB + JB, width), f32),
        pltpu.VMEM((IB + JB, width), f32),
        pltpu.VMEM((tiles, na, nb, rt, width), bf16),
        pltpu.VMEM((tiles, na, nc, rs, width), bf16),
        pltpu.VMEM((tiles, edge, width), bf16),
        pltpu.VMEM((tiles, edge, width), bf16),
        pltpu.VMEM((edge, width), bf16),
        pltpu.VMEM((edge, width), f32),
        pltpu.VMEM((tiles, edge, edge, width), bf16),
        pltpu.VMEM((edge, width), f32),
        pltpu.VMEM((tiles, nc - 1, nb, sh1, width), bf16),
        pltpu.VMEM((tiles, nc - 1, nb, sh1, width), bf16),
        pltpu.VMEM((tiles, nb, sh1, width), f32),
        pltpu.VMEM((tiles, nb - 1, sh1, width), bf16),
        pltpu.VMEM((tiles, nb - 1, sh1, width), bf16),
        pltpu.VMEM((tiles, sh1, width), f32),
        pltpu.VMEM((sh1, rank), bf16),
        pltpu.VMEM((tiles, nb, nc, sh1, width), bf16),
        pltpu.VMEM((tiles, nc - 1, na, sh2, width), bf16),
        pltpu.VMEM((tiles, nc - 1, na, sh2, width), bf16),
        pltpu.VMEM((tiles, na, sh2, width), f32),
        pltpu.VMEM((tiles, na - 1, sh2, width), bf16),
        pltpu.VMEM((tiles, na - 1, sh2, width), bf16),
        pltpu.VMEM((tiles, sh2, width), f32),
        pltpu.VMEM((sh2, rank), bf16),
        pltpu.SMEM(coordinates.shape, jnp.int32),
        pltpu.SMEM(occupancy.shape, jnp.int32),
        dma((2 * tiles + 5,)),
        dma((2,)),
        dma((2,)),
        dma((3, tiles, na - 1)),
        dma((3, tiles, na - 1)),
        dma((3, tiles, nb - 1)),
        dma((3, tiles, nb - 1)),
        dma((5, tiles, widest_k)),
        dma((5, tiles, widest_k)),
    ]
    results = pl.pallas_call(
        functools.partial(kernel, sizes),
        name="als",
        out_shape=(
            jax.ShapeDtypeStruct((1, sh1, rank), bf16),
            jax.ShapeDtypeStruct((1, sh2, rank), bf16),
        ),
        in_specs=[anywhere, anywhere, anywhere, vmem, vmem, anywhere, anywhere],
        out_specs=(vmem, vmem),
        scratch_shapes=scratch,
        compiler_params=pltpu.CompilerParams(
            collective_id=0, has_side_effects=True, vmem_limit_bytes=67043328
        ),
    )(blocks, coordinates, occupancy, second_factor, third_factor, inverse_first, inverse_second)
    return pl.pallas_call(
        hand_over,
        name="hand_over",
        out_shape=tuple(jax.ShapeDtypeStruct(x.shape, x.dtype) for x in results),
        in_specs=[vmem, vmem],
        out_specs=(vmem, vmem),
    )(*results)


def hand_over(first_in, second_in, first_out, second_out):
    first_out[...] = first_in[...]
    second_out[...] = second_in[...]


def solution(mesh):
    sizes = tuple(mesh.shape[name] for name in AXES)
    in_specs = (
        P("ia", "ja", "ka", None, None, None),
        P(None, "ia", "ja", "ka"),
        P("ia", "ja", "ka"),
        P("ja", ("ia", "ka"), None),
        P("ka", ("ia", "ja"), None),
        P(),
        P(),
    )
    out_specs = (P("ia", ("ja", "ka"), None), P("ja", ("ia", "ka"), None))
    return jax.shard_map(
        functools.partial(body, sizes),
        mesh=mesh,
        in_specs=in_specs,
        out_specs=out_specs,
        check_vma=False,
    )
```

profile of v0, /device:TPU:0, one launch (start us, length us, event | category | flops | bytes accessed | tf_op | source)
XLA Modules:
  0.0 74.0 jit_solution(5141574636573736816)
XLA Ops:
  0.6 1.3 %copy.9.places_in = s32[3,1,1,2]{3,2,1,0:T(1,128)} copy(s32[3,1,1,2]{0,3,2,1:T(2,128)} %param.8) | data formatting | bytes 48 | tf_op args[1]
  1.9 70.4 %als.1 = (bf16[1,64,1024]{2,1,0:T(8,128)(2,1)}, bf16[1,64,1024]{2,1,0:T(8,128)(2,1)}) custom-call(bf16[1,1,2,128,128,128]{5,4,3,2,1,0:T(8,128)(2,1)} %blocks.1, s32[3,1,1,2]{3,2,1,0:T(1,128)} %copy.9.places_in, s32[1,1,2]{2,1,0:T(1,128)} %occupied_in.1, bf16[1,64,1024]{2,1,0:T(8,128)(2,1)} %second_in.1, bf16[1,32,1024]{2,1,0:T(8,128)(2,1)} %third_in.1, ...), custom_call_target="tpu_custom_call" | custom-call | tf_op jit(solution)/shard_map/als/pallas_call | solution.py:499
  72.4 1.7 %hand_over.1 = (bf16[1,64,1024]{2,1,0:T(8,128)(2,1)}, bf16[1,64,1024]{2,1,0:T(8,128)(2,1)}) custom-call(bf16[1,64,1024]{2,1,0:T(8,128)(2,1)} %get-tuple-element.4.first_in, bf16[1,64,1024]{2,1,0:T(8,128)(2,1)} %get-tuple-element.5.second_in), custom_call_target="tpu_custom_call" | custom-call | tf_op jit(solution)/shard_map/hand_over/pallas_call | solution.py:513
where the time goes:
time: 74.2 us; the launch traced here: 74 us
  Pallas kernels  72.1 us (97%)
  local copies, waits for them, and re-layouts  1.32 us (2%)
    pallas_call x1, Pallas kernels, body(): pl.pallas_call(functools.partial(kernel, sizes), name='als', out_shape=(j...  70.4 us
    pallas_call x1, Pallas kernels, body(): pl.pallas_call(hand_over, name='hand_over', out_shape=tuple((jax.ShapeDty...  1.68 us

commit v1 on v0

v1 whole, which is shorter than its diff:
```python
import functools

import jax
import jax.numpy as jnp
from jax import lax
from jax.experimental import pallas as pl
from jax.experimental.pallas import tpu as pltpu
from jax.sharding import PartitionSpec as P

IB = 4
JB = 4
TILES = 4
GROUP = 32
MESH = pl.DeviceIdType.MESH
AXES = ("ia", "ja", "ka")


def kernel(
    sizes,
    blocks,
    places_in,
    occupied_in,
    second_in,
    third_in,
    inverse_first,
    inverse_second,
    first_out,
    second_out,
    xbuf,
    inv1,
    inv2,
    meta_s,
    meta_r,
    cbuf,
    bbuf,
    slab_s,
    slab_r,
    cuse,
    buse,
    tbuf,
    oacc,
    d1s,
    d1r,
    keep1,
    p1s,
    p1r,
    own1,
    total1,
    abuf,
    d2s,
    d2r,
    keep2,
    p2s,
    p2r,
    own2,
    total2,
    obuf,
    places,
    occupied,
    local_sem,
    once_send,
    once_recv,
    send_sem,
    recv_sem,
):
    na, nb, nc = sizes
    tiles, edge, width = slab_s.shape
    rs, rt = bbuf.shape[3], cbuf.shape[3]
    sh1, sh2 = abuf.shape[3], own2.shape[1]
    a, b, c = (lax.axis_index(name) for name in AXES)
    def away(axis, d):
        n = sizes[AXES.index(axis)]
        me = (a, b, c)[AXES.index(axis)]
        return lax.rem(me + d, n)

    def send(src, dst, send_sem, recv_sem, axis, d):
        copy = pltpu.make_async_remote_copy(
            src_ref=src,
            dst_ref=dst,
            send_sem=send_sem,
            recv_sem=recv_sem,
            device_id={axis: away(axis, d)},
            device_id_type=MESH,
        )
        copy.start()

    barrier = pltpu.get_barrier_semaphore()
    for axis, n in zip(AXES, sizes):
        for d in range(1, n):
            pl.semaphore_signal(
                barrier, inc=1, device_id={axis: away(axis, d)}, device_id_type=MESH
            )
    def cols(t):
        return pl.ds(t * width, width)

    def landed(ref, sem):
        pltpu.make_async_copy(ref, ref, sem).wait()

    def local_copy(src, dst, n):
        pltpu.make_async_copy(src, dst, local_sem.at[n]).start()

    local_copy(places_in, places, 0)
    local_copy(occupied_in, occupied, 1)
    for t in range(tiles):
        local_copy(third_in.at[0, :, cols(t)], cbuf.at[t, a, b], 2)
        local_copy(second_in.at[0, :, cols(t)], bbuf.at[t, a, c], 3)
    local_copy(blocks.at[0, 0, 0], xbuf.at[0], 4)
    local_copy(inverse_first, inv1, 5)
    local_copy(inverse_second, inv2, 6)
    landed(places, local_sem.at[0])
    landed(occupied, local_sem.at[1])
    keep = occupied[0, 0, 0] > 0
    row0, col0, layer0 = (places[0, 0, 0, m] for m in range(3))
    row1, col1, layer1 = (places[0, 0, 1, m] for m in range(3))
    weight1 = jnp.where(occupied[0, 0, 1] > 0, 1.0, 0.0).astype(jnp.float32)
    for q in range(IB):
        value = jnp.where(row1 == q, weight1, 0.0)
        meta_s[pl.ds(q, 1), :] = jnp.full((1, width), value, jnp.float32)
    for q in range(JB):
        value = jnp.where(col1 == q, weight1, 0.0)
        meta_s[pl.ds(IB + q, 1), :] = jnp.full((1, width), value, jnp.float32)
    pl.semaphore_wait(barrier, (na - 1) + (nb - 1) + (nc - 1))

    def chosen(own_value, row):
        own = jnp.where(own_value, 1.0, 0.0).astype(jnp.float32)
        return jnp.where(keep, jnp.full((1, width), own, jnp.float32), meta_r[pl.ds(row, 1), :]) > 0.5

    def third_column(t):
        for d in range(1, na):
            send(
                third_in.at[0, :, cols(t)],
                cbuf.at[t, a, b],
                send_sem.at[0],
                recv_sem.at[0, t],
                "ia",
                d,
            )

    def second_column(t):
        for d in range(1, na):
            send(
                second_in.at[0, :, cols(t)],
                bbuf.at[t, a, c],
                send_sem.at[1],
                recv_sem.at[1, t],
                "ia",
                d,
            )

    third_column(0)
    send(blocks.at[0, 0, 1], xbuf.at[1], once_send.at[0], once_recv.at[0], "ka", 1)
    send(meta_s, meta_r, once_send.at[1], once_recv.at[1], "ka", 1)
    for t in range(1, tiles):
        third_column(t)
        second_column(t - 1)
    second_column(tiles - 1)

    def spread_third(t):
        if t == 0:
            landed(cbuf.at[:, a, b], local_sem.at[2])
        landed(cbuf.at[t, pl.ds(0, na - 1), b], recv_sem.at[0, t])
        for d in range(1, nb):
            send(
                cbuf.at[t, :, b],
                cbuf.at[t, :, b],
                send_sem.at[2],
                recv_sem.at[2, t],
                "ja",
                d,
            )

    def spread_second(t):
        if t == 0:
            landed(bbuf.at[:, a, c], local_sem.at[3])
        landed(bbuf.at[t, pl.ds(0, na - 1), c], recv_sem.at[1, t])
        for d in range(1, nc):
            send(
                bbuf.at[t, :, c],
                bbuf.at[t, :, c],
                send_sem.at[3],
                recv_sem.at[3, t],
                "ka",
                d,
            )

    def layer_piece(t, layer, piece):
        per = edge // rt
        total = na * nb * rt // edge
        value = None
        for q in range(total):
            s = q * per + piece
            rows = cbuf[t, s // nb, s % nb]
            value = rows if value is None else jnp.where(layer == q, rows, value)
        return value

    def pass_slab(t):
        landed(cbuf.at[t, :, pl.ds(0, nb - 1)], recv_sem.at[2, t])
        for piece in range(edge // rt):
            slab_s[t, pl.ds(piece * rt, rt), :] = layer_piece(t, layer1, piece)
        send(slab_s.at[t], slab_r.at[t], send_sem.at[4], recv_sem.at[4, t], "ka", 1)

    def first_products(t, between):
        for piece in range(edge // rt):
            cuse[pl.ds(piece * rt, rt), :] = layer_piece(t, layer0, piece)
        landed(bbuf.at[t, :, pl.ds(0, nc - 1)], recv_sem.at[3, t])
        if t == 0:
            landed(xbuf.at[0], local_sem.at[4])
            landed(xbuf.at[1], once_recv.at[0])
            landed(meta_r, once_recv.at[1])
        masks = [chosen(col0 == q, IB + q) for q in range(JB)]
        per = edge // rs
        for piece in range(per):
            value = jnp.zeros((rs, width), jnp.float32)
            for q in range(JB):
                s = q * per + piece
                rows = bbuf[t, s // nc, s % nc].astype(jnp.float32)
                value = jnp.where(masks[q], rows, value)
            buse[pl.ds(piece * rs, rs), :] = value
        landed(slab_r.at[t], recv_sem.at[4, t])
        cuse[...] = jnp.where(keep, cuse[...], slab_r[t])
        slot = jnp.where(keep, 0, 1)

        def several(step, carry):
            base = pl.multiple_of(step * GROUP, GROUP)
            left = xbuf[slot, pl.ds(base, GROUP)].reshape(GROUP * edge, edge)
            product = jnp.dot(left, cuse[...], preferred_element_type=jnp.float32)
            sums = []
            for u in range(GROUP):
                part = product[u * edge : (u + 1) * edge]
                tbuf[t, base + u] = part.astype(jnp.bfloat16)
                sums.append(jnp.sum(part * buse[...], axis=0, keepdims=True))
            oacc[pl.ds(base, GROUP), :] = jnp.concatenate(sums, axis=0)
            return carry

        steps = edge // GROUP
        lax.fori_loop(0, steps // 2, several, 0)
        between()
        lax.fori_loop(steps // 2, steps, several, 0)

    def owned_piece(owner, rows, own_place, meta_row):
        start = owner * rows
        block = start // edge
        off = pl.multiple_of(start % edge, rows)
        mask = chosen(own_place == block, meta_row + block)
        return jnp.where(mask, oacc[pl.ds(off, rows), :], 0.0)

    def pair_sums(t, n, rows, own_place, meta_row, outgoing, arriving, kept, kind):
        for d in range(1, nc):
            for m in range(n):
                owner = m * nc + away("ka", d)
                outgoing[t, d - 1, m] = owned_piece(owner, rows, own_place, meta_row).astype(
                    jnp.bfloat16
                )
            send(
                outgoing.at[t, d - 1],
                arriving.at[t, d - 1],
                send_sem.at[kind],
                recv_sem.at[kind, t],
                "ka",
                d,
            )
        for m in range(n):
            kept[t, m] = owned_piece(m * nc + c, rows, own_place, meta_row)

    def chip_sums(t, axis, n, arriving, kept, outgoing, landing, own, pair, kind):
        landed(arriving.at[t], recv_sem.at[pair, t])
        for d in range(n):
            m = away(axis, d)
            value = kept[t, m]
            for e in range(1, nc):
                value = value + arriving[t, e - 1, m].astype(jnp.float32)
            if d == 0:
                own[t] = value
            else:
                outgoing[t, d - 1] = value.astype(jnp.bfloat16)
                send(
                    outgoing.at[t, d - 1],
                    landing.at[t, d - 1],
                    send_sem.at[kind],
                    recv_sem.at[kind, t],
                    axis,
                    d,
                )

    def first_chip_sums(t):
        chip_sums(t, "ja", nb, d1r, keep1, p1s, p1r, own1, 5, 6)

    def gathered(t, own, landing, n, kind):
        landed(landing.at[t], recv_sem.at[kind, t])
        value = own[t]
        for d in range(1, n):
            value = value + landing[t, d - 1].astype(jnp.float32)
        return value.astype(jnp.bfloat16)

    def fold(t, value, inverse, total):
        part = jnp.dot(value, inverse[cols(t), :], preferred_element_type=jnp.float32)
        total[...] = part if t == 0 else total[...] + part

    def first_fold(t):
        fold(t, gathered(t, own1, p1r, nb, 6), inv1, total1)

    spread_third(0)
    if tiles > 1:
        spread_third(1)
    spread_second(0)
    pass_slab(0)
    for t in range(tiles):

        def between(t=t):
            if t + 1 < tiles:
                spread_second(t + 1)
                pass_slab(t + 1)
            if t:
                first_chip_sums(t - 1)

        first_products(t, between)
        pair_sums(t, nb, sh1, row0, 0, d1s, d1r, keep1, 5)
        if t + 2 < tiles:
            spread_third(t + 2)
        if t == 1:
            landed(inv1, local_sem.at[5])
        if t > 1:
            first_fold(t - 2)
    first_chip_sums(tiles - 1)
    for t in range(max(tiles - 2, 0), tiles):
        first_fold(t)
    for t in range(tiles):
        abuf[t, b, c] = total1[:, cols(t)].astype(jnp.bfloat16)
        for d in range(1, nb):
            send(
                abuf.at[t, b, c],
                abuf.at[t, b, c],
                send_sem.at[7],
                recv_sem.at[7, t],
                "ja",
                d,
            )
    for t in range(tiles):
        local_copy(abuf.at[t, b, c], first_out.at[0, :, cols(t)], 7)

    def spread_new(t):
        landed(abuf.at[t, pl.ds(0, nb - 1), c], recv_sem.at[7, t])
        for d in range(1, nc):
            send(
                abuf.at[t, :, c],
                abuf.at[t, :, c],
                send_sem.at[8],
                recv_sem.at[8, t],
                "ka",
                d,
            )

    def second_products(t):
        landed(abuf.at[t, :, pl.ds(0, nc - 1)], recv_sem.at[8, t])
        masks = [chosen(row0 == q, q) for q in range(IB)]
        per = edge // sh1
        for piece in range(per):
            value = jnp.zeros((sh1, width), jnp.float32)
            for q in range(IB):
                s = q * per + piece
                rows = abuf[t, s // nc, s % nc].astype(jnp.float32)
                value = jnp.where(masks[q], rows, value)
            buse[pl.ds(piece * sh1, sh1), :] = value
        lanes = 128
        for lane in range(0, width, lanes):

            def eight(step, total):
                base = pl.multiple_of(step * 8, 8)
                rows = buse[pl.ds(base, 8), pl.ds(lane, lanes)]
                for u in range(8):
                    total = total + rows[u : u + 1] * tbuf[t, base + u, :, pl.ds(lane, lanes)].astype(
                        jnp.float32
                    )
                return total

            oacc[:, pl.ds(lane, lanes)] = lax.fori_loop(
                0, edge // 8, eight, jnp.zeros((edge, lanes), jnp.float32)
            )

    def second_chip_sums(t):
        chip_sums(t, "ia", na, d2r, keep2, p2s, p2r, own2, 9, 10)

    def second_fold(t):
        fold(t, gathered(t, own2, p2r, na, 10), inv2, total2)

    spread_new(0)
    for t in range(tiles):
        if t + 1 < tiles:
            spread_new(t + 1)
        second_products(t)
        pair_sums(t, na, sh2, col0, IB, d2s, d2r, keep2, 9)
        if t:
            second_chip_sums(t - 1)
        if t == 1:
            landed(inv2, local_sem.at[6])
        if t > 1:
            second_fold(t - 2)
    second_chip_sums(tiles - 1)
    for t in range(max(tiles - 2, 0), tiles):
        second_fold(t)
    obuf[...] = total2[...].astype(jnp.bfloat16)
    local_copy(obuf, second_out.at[0], 8)
    landed(blocks.at[0, 0, 1], once_send.at[0])
    landed(meta_s, once_send.at[1])
    landed(cbuf.at[:, pl.ds(0, na - 1), b], send_sem.at[0])
    landed(bbuf.at[:, pl.ds(0, na - 1), c], send_sem.at[1])
    landed(cbuf.at[:, :, pl.ds(0, nb - 1)], send_sem.at[2])
    landed(bbuf.at[:, :, pl.ds(0, nc - 1)], send_sem.at[3])
    landed(slab_s, send_sem.at[4])
    landed(d1s, send_sem.at[5])
    landed(p1s, send_sem.at[6])
    landed(abuf.at[:, pl.ds(0, nb - 1), c], send_sem.at[7])
    landed(abuf.at[:, :, pl.ds(0, nc - 1)], send_sem.at[8])
    landed(d2s, send_sem.at[9])
    landed(p2s, send_sem.at[10])
    landed(first_out.at[0], local_sem.at[7])
    landed(second_out.at[0], local_sem.at[8])


def body(
    sizes,
    blocks,
    coordinates,
    occupancy,
    second_factor,
    third_factor,
    inverse_first,
    inverse_second,
):
    coordinates = jnp.transpose(coordinates, (1, 2, 3, 0))
    na, nb, nc = sizes
    edge, rank = blocks.shape[-1], inverse_first.shape[0]
    tiles = TILES
    width = rank // tiles
    rs, rt = second_factor.shape[1], third_factor.shape[1]
    sh1, sh2 = IB * edge // (nb * nc), JB * edge // (na * nc)
    bf16, f32 = jnp.bfloat16, jnp.float32
    dma = pltpu.SemaphoreType.DMA
    vmem = pl.BlockSpec(memory_space=pltpu.VMEM)
    anywhere = pl.BlockSpec(memory_space=pl.ANY)
    scratch = [
        pltpu.VMEM((2, edge, edge, edge), bf16),
        pltpu.VMEM((rank, rank), bf16),
        pltpu.VMEM((rank, rank), bf16),
        pltpu.VMEM((IB + JB, width), f32),
        pltpu.VMEM((IB + JB, width), f32),
        pltpu.VMEM((tiles, na, nb, rt, width), bf16),
        pltpu.VMEM((tiles, na, nc, rs, width), bf16),
        pltpu.VMEM((tiles, edge, width), bf16),
        pltpu.VMEM((tiles, edge, width), bf16),
        pltpu.VMEM((edge, width), bf16),
        pltpu.VMEM((edge, width), f32),
        pltpu.VMEM((tiles, edge, edge, width), bf16),
        pltpu.VMEM((edge, width), f32),
        pltpu.VMEM((tiles, nc - 1, nb, sh1, width), bf16),
        pltpu.VMEM((tiles, nc - 1, nb, sh1, width), bf16),
        pltpu.VMEM((tiles, nb, sh1, width), f32),
        pltpu.VMEM((tiles, nb - 1, sh1, width), bf16),
        pltpu.VMEM((tiles, nb - 1, sh1, width), bf16),
        pltpu.VMEM((tiles, sh1, width), f32),
        pltpu.VMEM((sh1, rank), f32),
        pltpu.VMEM((tiles, nb, nc, sh1, width), bf16),
        pltpu.VMEM((tiles, nc - 1, na, sh2, width), bf16),
        pltpu.VMEM((tiles, nc - 1, na, sh2, width), bf16),
        pltpu.VMEM((tiles, na, sh2, width), f32),
        pltpu.VMEM((tiles, na - 1, sh2, width), bf16),
        pltpu.VMEM((tiles, na - 1, sh2, width), bf16),
        pltpu.VMEM((tiles, sh2, width), f32),
        pltpu.VMEM((sh2, rank), f32),
        pltpu.VMEM((sh2, rank), bf16),
        pltpu.SMEM(coordinates.shape, jnp.int32),
        pltpu.SMEM(occupancy.shape, jnp.int32),
        dma((9,)),
        dma((2,)),
        dma((2,)),
        dma((11,)),
        dma((11, tiles)),
    ]
    results = pl.pallas_call(
        functools.partial(kernel, sizes),
        name="als",
        out_shape=(
            jax.ShapeDtypeStruct((1, sh1, rank), bf16),
            jax.ShapeDtypeStruct((1, sh2, rank), bf16),
        ),
        in_specs=[anywhere, anywhere, anywhere, vmem, vmem, anywhere, anywhere],
        out_specs=(anywhere, anywhere),
        scratch_shapes=scratch,
        compiler_params=pltpu.CompilerParams(
            collective_id=0, has_side_effects=True, vmem_limit_bytes=67043328
        ),
    )(blocks, coordinates, occupancy, second_factor, third_factor, inverse_first, inverse_second)
    return pl.pallas_call(
        hand_over,
        name="hand_over",
        out_shape=tuple(jax.ShapeDtypeStruct(x.shape, x.dtype) for x in results),
        in_specs=[vmem, vmem],
        out_specs=(vmem, vmem),
    )(*results)


def hand_over(first_in, second_in, first_out, second_out):
    first_out[...] = first_in[...]
    second_out[...] = second_in[...]


def solution(mesh):
    sizes = tuple(mesh.shape[name] for name in AXES)
    in_specs = (
        P("ia", "ja", "ka", None, None, None),
        P(None, "ia", "ja", "ka"),
        P("ia", "ja", "ka"),
        P("ja", ("ia", "ka"), None),
        P("ka", ("ia", "ja"), None),
        P(),
        P(),
    )
    out_specs = (P("ia", ("ja", "ka"), None), P("ja", ("ia", "ka"), None))
    return jax.shard_map(
        functools.partial(body, sizes),
        mesh=mesh,
        in_specs=in_specs,
        out_specs=out_specs,
        check_vma=False,
    )
```

time: 74.2 us -> 71.6 us (0.965)
  local copies, waits for them, and re-layouts: 1.32 us -> 0 us
  Pallas kernels: 72.1 us -> 70.8 us
    unnamed x1 -> x0, local copies, waits for them, and re-layouts: 1.32 us -> none
    pallas_call x1, Pallas kernels: 70.4 us -> 69.1 us  [body(): pl.pallas_call(functools.partial(kernel, sizes), name='als', out_shape=(j...]
where the time goes in v1:
time: 71.6 us; the launch traced here: 71.4 us
  Pallas kernels  70.8 us (99%)
    pallas_call x1, Pallas kernels, body(): pl.pallas_call(functools.partial(kernel, sizes), name='als', out_shape=(j...  69.1 us
    pallas_call x1, Pallas kernels, body(): pl.pallas_call(hand_over, name='hand_over', out_shape=tuple((jax.ShapeDty...  1.68 us

profile of v1, /device:TPU:0, one launch (start us, length us, event | category | flops | bytes accessed | tf_op | source)
XLA Modules:
  0.0 71.4 jit_solution(18423312454462108650)
XLA Ops:
  0.6 69.1 %als.1 = (bf16[1,64,1024]{2,1,0:T(8,128)(2,1)}, bf16[1,64,1024]{2,1,0:T(8,128)(2,1)}) custom-call(bf16[1,1,2,128,128,128]{5,4,3,2,1,0:T(8,128)(2,1)} %blocks.1, s32[1,1,2,3]{3,2,1,0:T(2,128)} %bitcast.1, s32[1,1,2]{2,1,0:T(1,128)} %occupied_in.1, bf16[1,64,1024]{2,1,0:T(8,128)(2,1)} %second_in.1, bf16[1,32,1024]{2,1,0:T(8,128)(2,1)} %third_in.1, ...), custom_call_target="tpu_custom_call" | custom-call | tf_op jit(solution)/shard_map/als/pallas_call | solution.py:479
  69.7 1.7 %hand_over.1 = (bf16[1,64,1024]{2,1,0:T(8,128)(2,1)}, bf16[1,64,1024]{2,1,0:T(8,128)(2,1)}) custom-call(bf16[1,64,1024]{2,1,0:T(8,128)(2,1)} %get-tuple-element.4.first_in, bf16[1,64,1024]{2,1,0:T(8,128)(2,1)} %get-tuple-element.5.second_in), custom_call_target="tpu_custom_call" | custom-call | tf_op jit(solution)/shard_map/hand_over/pallas_call | solution.py:493
